TPU v7x, 128 devices: a whole 4x4x4 slice. The times are simulated.
128 devices in a mesh: tok: 32 (over y, x, core), mlp: 4 (over z).
Axes of the slice: x: 4, y: 4, z: 4, core: 2. Of those that a mesh axis runs over, the one named last changes fastest.
Arguments:
- layer_input: bfloat16 [16384, 4096], P('tok'), may hold values from -80 to 80
- input_norm_gain: float32 [4096], replicated, may hold values from 0.6 to 10
- query_weight: bfloat16 [4096, 4096], P(None, 'mlp'), may hold values from -0.09375 to 0.09375
- key_weight: bfloat16 [4096, 1024], P(None, 'mlp'), may hold values from -0.09375 to 0.09375
- value_weight: bfloat16 [4096, 1024], P(None, 'mlp'), may hold values from -0.09375 to 0.09375
- query_down_maps: bfloat16 [256, 16, 4096], P('tok', None, 'mlp'), may hold values from -0.09375 to 0.09375
- value_down_maps: bfloat16 [256, 16, 4096], P('tok', None, 'mlp'), may hold values from -0.09375 to 0.09375
- query_up_maps: bfloat16 [256, 16, 4096], P('tok', None, 'mlp'), may hold values from -1.5 to 1.5
- value_up_maps: bfloat16 [256, 16, 1024], P('tok', None, 'mlp'), may hold values from -1.5 to 1.5
- tenant_prompt_length: int32 [16], replicated, may hold values from 1 to 2048, 16384 in all
- tenant_adapter_id: int32 [16], replicated, may hold values from 0 to 255
- adapter_storage_slot: int32 [256], replicated, may hold values from 0 to 255, each once
Outputs:
- attended: bfloat16 [16384, 4096], P('tok', 'mlp')
Inputs may be any that keep to these rules, and one draw needn't show every extreme that they name: `tenant_prompt_length`: the lengths sum to 16384; each is at most 2048 and one of them is exactly that. `tenant_adapter_id`: tenants may share an adapter. `adapter_storage_slot`: each storage slot holds exactly one adapter.
All inputs are finite; a program needn't handle non-finite values.
Results may differ from a plain program's by a relative error of at most 0.0045.
The roundings to bfloat16 on the way count: a program that leaves them out, or rounds other values in their place, can miss the bound.
Values may be sent and summed in bfloat16 or wider, within the bound.
A program may use at most 192 MiB of HBM per device.

v0:
```python
import jax
import jax.numpy as jnp
from jax import lax
from jax.sharding import PartitionSpec as P

HEAD_WIDTH = 128
ADAPTER_RANK = 16
LONGEST_PROMPT = 4
NORM_EPS = 1e-05
ROPE_BASE = 500000.0
ADAPTER_SCALE = 0.5


def from_behind(x, axis, by):
    peers = lax.axis_size(axis)
    pairs = [(i, i + by) for i in range(peers) if 0 <= i + by < peers]
    return lax.ppermute(x, axis, pairs)


def rotary(values, positions):
    half_width = values.shape[-1] // 2
    exponent = jnp.arange(half_width).astype(jnp.float32) * (2.0 / values.shape[-1])
    inverse = jnp.exp(-exponent * jnp.log(jnp.float32(ROPE_BASE)))
    angles = positions.astype(jnp.float32)[:, None] * inverse[None, :]
    cosine = jnp.cos(angles)[:, None, :]
    sine = jnp.sin(angles)[:, None, :]
    first_position = values[..., :half_width]
    second = values[..., half_width:]
    return jnp.concatenate(
        [first_position * cosine - second * sine, second * cosine + first_position * sine], axis=-1
    )


def tenant_of(tenant_prompt_length, indices):
    prompt_ends = jnp.cumsum(tenant_prompt_length)
    prompt_starts = prompt_ends - tenant_prompt_length
    tenant_ids = jnp.sum((indices[:, None] >= prompt_ends[None, :]).astype(jnp.int32), axis=1)
    member = (
        tenant_ids[:, None] == jnp.arange(tenant_prompt_length.shape[0], dtype=jnp.int32)[None, :]
    )
    row_start = jnp.sum(jnp.where(member, prompt_starts[None, :], 0), axis=1)
    return (member, row_start)


def contract(left, table):
    flat = table.reshape(-1, table.shape[2])
    return lax.dot_general(left, flat, (((1,), (1,)), ((), ())), preferred_element_type=jnp.float32)


def body(
    layer_input,
    input_norm_gain,
    query_weight,
    key_weight,
    value_weight,
    query_down_maps,
    value_down_maps,
    query_up_maps,
    value_up_maps,
    tenant_prompt_length,
    tenant_adapter_id,
    adapter_storage_slot,
):
    tok_rows = layer_input.shape[0]
    device = lax.axis_index("tok")
    held_tokens = query_down_maps.shape[0]
    catalog = adapter_storage_slot.shape[0]
    matches = tenant_adapter_id[:, None] == jnp.arange(catalog, dtype=jnp.int32)[None, :]
    storage_slots = jnp.sum(jnp.where(matches, adapter_storage_slot[None, :], 0), axis=1)
    local_slot = storage_slots - device * held_tokens
    picker = (local_slot[:, None] == jnp.arange(held_tokens, dtype=jnp.int32)[None, :]).astype(
        jnp.bfloat16
    )

    def selector(stored):
        return jnp.einsum("th,hrc->trc", picker, stored, preferred_element_type=jnp.float32)

    summed = (
        lax.psum(selector(query_down_maps).astype(jnp.bfloat16), "tok").astype(jnp.float32),
        lax.psum(selector(value_down_maps).astype(jnp.bfloat16), "tok").astype(jnp.float32),
        lax.psum(selector(query_up_maps).astype(jnp.bfloat16), "tok").astype(jnp.float32),
        lax.psum(selector(value_up_maps).astype(jnp.bfloat16), "tok").astype(jnp.float32),
    )
    query_down_table = summed[0].astype(jnp.bfloat16)
    value_down_table = summed[1].astype(jnp.bfloat16)
    query_up_table = summed[2].astype(jnp.bfloat16)
    value_up_table = summed[3].astype(jnp.bfloat16)
    widened = layer_input.astype(jnp.float32)
    scale_row = lax.rsqrt(jnp.mean(widened * widened, axis=1, keepdims=True) + NORM_EPS)
    normed_input = (widened * scale_row * input_norm_gain[None, :]).astype(jnp.bfloat16)
    indices = device * tok_rows + jnp.arange(tok_rows, dtype=jnp.int32)
    member, row_start = tenant_of(tenant_prompt_length, indices)
    positions = indices - row_start
    chosen = jnp.repeat(member, ADAPTER_RANK, axis=1)
    full_aq, full_av = (
        lax.all_gather(query_down_table, "mlp", axis=2, tiled=True),
        lax.all_gather(value_down_table, "mlp", axis=2, tiled=True),
    )
    shrink_q = contract(normed_input, full_aq)
    shrink_v = contract(normed_input, full_av)
    shrink_q = jnp.where(chosen, shrink_q, 0.0).astype(jnp.bfloat16)
    shrink_v = jnp.where(chosen, shrink_v, 0.0).astype(jnp.bfloat16)
    query_delta = jnp.dot(
        shrink_q,
        query_up_table.reshape(-1, query_up_table.shape[2]),
        preferred_element_type=jnp.float32,
    )
    value_delta = jnp.dot(
        shrink_v,
        value_up_table.reshape(-1, value_up_table.shape[2]),
        preferred_element_type=jnp.float32,
    )
    query_rows = (
        jnp.dot(normed_input, query_weight, preferred_element_type=jnp.float32)
        + ADAPTER_SCALE * query_delta
    )
    query_rows = rotary(query_rows.reshape(tok_rows, -1, HEAD_WIDTH), positions).astype(
        jnp.bfloat16
    )
    key = jnp.dot(normed_input, key_weight, preferred_element_type=jnp.float32)
    key = rotary(key.reshape(tok_rows, -1, HEAD_WIDTH), positions).astype(jnp.bfloat16)
    value_rows = (
        jnp.dot(normed_input, value_weight, preferred_element_type=jnp.float32)
        + ADAPTER_SCALE * value_delta
    )
    value_rows = value_rows.astype(jnp.bfloat16).reshape(tok_rows, -1, HEAD_WIDTH)
    key_blocks = []
    value_blocks = []
    for shift_by in range(LONGEST_PROMPT, 0, -1):
        moved_key, moved_value = from_behind((key, value_rows), "tok", shift_by)
        key_blocks.append(moved_key)
        value_blocks.append(moved_value)
    key_blocks.append(key)
    value_blocks.append(value_rows)
    all_values = jnp.concatenate(value_blocks, axis=0)
    span = (LONGEST_PROMPT + 1) * tok_rows
    k_index = (device - LONGEST_PROMPT) * tok_rows + jnp.arange(span, dtype=jnp.int32)
    allowed = (k_index[None, :] >= row_start[:, None]) & (k_index[None, :] <= indices[:, None])
    heads_here = query_rows.shape[1]
    kv_here = key.shape[1]
    head_groups = heads_here // kv_here
    outputs = []
    for kv_group in range(kv_here):
        q_group = query_rows[:, kv_group * head_groups : (kv_group + 1) * head_groups, :]
        pieces = []
        for block_index in range(LONGEST_PROMPT + 1):
            block_keys = key_blocks[block_index][:, kv_group, :]

            def dense_scores(q_group=q_group, block_keys=block_keys):
                return jnp.einsum(
                    "qgd,kd->gqk", q_group, block_keys, preferred_element_type=jnp.float32
                )

            pieces.append(dense_scores())
        scores = jnp.concatenate(pieces, axis=2) * HEAD_WIDTH ** (-0.5)
        scores = jnp.where(allowed[None], scores, -jnp.inf)
        peak = jnp.max(scores, axis=-1, keepdims=True)
        weights = jnp.exp(scores - peak)
        totals = jnp.sum(weights, axis=-1)
        probs = weights.astype(jnp.bfloat16)
        mixed = jnp.einsum(
            "gqk,kd->qgd", probs, all_values[:, kv_group, :], preferred_element_type=jnp.float32
        )
        outputs.append(mixed / jnp.transpose(totals)[:, :, None])
    attended = jnp.concatenate(outputs, axis=1).astype(jnp.bfloat16)
    return attended.reshape(tok_rows, heads_here * HEAD_WIDTH)


def solution(mesh):
    placed = (
        P("tok", None),
        P(),
        P(None, "mlp"),
        P(None, "mlp"),
        P(None, "mlp"),
        P("tok", None, "mlp"),
        P("tok", None, "mlp"),
        P("tok", None, "mlp"),
        P("tok", None, "mlp"),
        P(),
        P(),
        P(),
    )
    return jax.shard_map(
        body, mesh=mesh, in_specs=placed, out_specs=P("tok", "mlp"), check_vma=False
    )
```

profile of v0, /device:TPU:1, one launch (start us, length us, event | category | flops | bytes accessed | tf_op | source)
XLA Modules:
  0.0 289.7 jit_solution(7563186682735671526)
XLA Ops:
  11.7 2.1 convolution_convert_fusion.1
  13.8 2.1 convolution_convert_fusion.2
  16.3 3.1 %fusion.12 = f32[512]{0:T(512)S(1)} fusion(bf16[512,4096]{1,0:T(8,128)(2,1)} %param.12), kind=kLoop, calls=%fused_computation.16 | loop fusion | flops 6290944 | bytes 4196352 | tf_op jit(solution)/shard_map/reduce_sum | solution.py:89
  19.4 106.0 %all-reduce.3.cloned.1.call-done = (bf16[256,1024]{1,0:T(8,128)(2,1)}, bf16[16,16,1024]{2,0,1:T(8,128)(2,1)}, bf16[256,256]{1,0:T(8,128)(2,1)}, bf16[16,16,1024]{2,0,1:T(8,128)(2,1)}) async-done(((bf16[256,1024]{1,0:T(8,128)(2,1)}, bf16[16,16,1024]{2,0,1:T(8,128)(2,1)}, bf16[256,256]{1,0:T(8,128)(2,1)}, bf16[16,16,1024]{2,0,1:T(8,128)(2,1)}), (bf16[256,1024]{1,0:T(8,128)(2,1)}, ...) | async-done | bytes 1703952 | tf_op jit(solution)/shard_map/psum | solution.py:81
  125.5 3.8 %fusion.14 = bf16[512,4096]{1,0:T(8,128)(2,1)S(1)} fusion(bf16[512,4096]{1,0:T(8,128)(2,1)} %param.12, f32[4096]{0:T(1024)S(1)} %copy-done.15, f32[512]{0:T(512)S(1)} %add_rsqrt_fusion), kind=kLoop, calls=%fused_computation.18 | loop fusion | flops 8388608 | bytes 8407040 | tf_op jit(solution)/shard_map/convert_element_type | solution.py:90
  129.3 1.9 copy-done.2
  136.0 3.1 %collective-permute-start.7 = (bf16[512,2,128]{2,0,1:T(8,128)(2,1)}, bf16[512,2,128]{2,0,1:T(8,128)(2,1)}, u32[]{:S(2)}, u32[]{:S(2)}) collective-permute-start(bf16[512,2,128]{2,0,1:T(8,128)(2,1)} %pad_maximum_fusion.2), channel_id=1, source_target_pairs={{0,4},{4,8},{8,12},{12,16},{16,20},{20,24},{24,28},{28,32},{32,36}... | collective-permute-start | bytes 786440 | tf_op jit(solution)/shard_map/ppermute | solution.py:17
  139.1 3.8 %collective-permute-start.6 = (bf16[512,2,128]{2,0,1:T(8,128)(2,1)}, bf16[512,2,128]{2,0,1:T(8,128)(2,1)}, u32[]{:S(2)}, u32[]{:S(2)}) collective-permute-start(bf16[512,2,128]{2,0,1:T(8,128)(2,1)} %pad_maximum_fusion.2), channel_id=1, source_target_pairs={{0,8},{4,12},{8,16},{12,20},{16,24},{20,28},{24,32},{28,36},{32,40... | collective-permute-start | bytes 786440 | tf_op jit(solution)/shard_map/ppermute | solution.py:17
  142.9 4.9 %collective-permute-start.5 = (bf16[512,2,128]{2,0,1:T(8,128)(2,1)}, bf16[512,2,128]{2,0,1:T(8,128)(2,1)}, u32[]{:S(2)}, u32[]{:S(2)}) collective-permute-start(bf16[512,2,128]{2,0,1:T(8,128)(2,1)} %pad_maximum_fusion.2), channel_id=1, source_target_pairs={{0,12},{4,16},{8,20},{12,24},{16,28},{20,32},{24,36},{28,40},{32,4... | collective-permute-start | bytes 786440 | tf_op jit(solution)/shard_map/ppermute | solution.py:17
  147.9 2.0 collective-permute-start.4
  150.2 5.1 %fusion.61 = f32[512,256]{0,1:T(8,128)} fusion(bf16[512,4096]{1,0:T(8,128)(2,1)} %copy-done.2, bf16[4096,256]{1,0:T(8,128)(2,1)} %param.16), kind=kOutput, calls=%fused_computation.114 | convolution fusion | flops 1073741824 | bytes 6815744 | tf_op jit(solution)/shard_map/dot_general | solution.py:123
  156.7 8.3 %fusion.63 = f32[512,1024]{1,0:T(8,128)} fusion(bf16[512,4096]{1,0:T(8,128)(2,1)S(1)} %copy-done.3, bf16[4096,1024]{1,0:T(8,128)(2,1)} %param.14), kind=kOutput, calls=%fused_computation.116 | convolution fusion | flops 4294967296 | bytes 14680064 | tf_op jit(solution)/shard_map/dot_general | solution.py:114
  165.0 2.7 copy.43
  167.7 4.9 %fusion.24 = bf16[512,256]{0,1:T(8,128)(2,1)} fusion(f32[512,256]{0,1:T(8,128)} %fusion.61, bf16[256,256]{1,0:T(8,128)(2,1)} %get-tuple-element.9, pred[512,256]{1,0:T(32,128)(4,1)S(1)} %copy.44, bf16[512,4096]{1,0:T(8,128)(2,1)} %copy-done.2, bf16[256,4096]{1,0:T(8,128)(2,1)S(1)} %bitcast.121), kind=kOutput, calls=%fused_computation.44 | convolution fusion | flops 1141506048 | bytes 7340032 | tf_op jit(solution)/shard_map/dot_general | solution.py:108
  172.6 3.3 %collective-permute-start.3 = (bf16[512,2,128]{0,2,1:T(8,128)(2,1)}, bf16[512,2,128]{0,2,1:T(8,128)(2,1)}, u32[]{:S(2)}, u32[]{:S(2)}) collective-permute-start(bf16[512,2,128]{0,2,1:T(8,128)(2,1)} %bitcast.126), channel_id=1, source_target_pairs={{0,4},{4,8},{8,12},{12,16},{16,20},{20,24},{24,28},{28,32},{32,36}... | collective-permute-start | bytes 786440 | tf_op jit(solution)/shard_map/ppermute | solution.py:17
  175.9 14.5 %all-gather.5.cloned.1.call-done = bf16[16,16,4096]{2,0,1:T(8,128)(2,1)} async-done(((bf16[16,16,1024]{2,0,1:T(8,128)(2,1)}), bf16[16,16,4096]{2,0,1:T(8,128)(2,1)}) %all-gather.5.cloned.1.call-update) | async-done | bytes 2097168 | tf_op jit(solution)/shard_map/all_gather | solution.py:96
  190.4 2.7 copy.50
  193.2 6.5 %add_bitcast_fusion = f32[64,8,8,128]{3,1,2,0:T(8,128)} fusion(f32[512,1024]{1,0:T(8,128)} %fusion.63, bf16[256,1024]{1,0:T(8,128)(2,1)} %get-tuple-element.7, pred[512,256]{1,0:T(32,128)(4,1)S(1)} %copy.44, bf16[512,4096]{1,0:T(8,128)(2,1)} %copy-done.2, bf16[256,4096]{1,0:T(8,128)(2,1)S(1)} %bitcast.119), kind=kOutput, calls=%fused_computation.32 | convolution fusion | flops 1343488000 | bytes 11141120 | tf_op jit(solution)/shard_map/dot_general | solution.py:103
  199.7 2.1 copy.65
  204.2 3.1 %collective-permute-start.2 = (bf16[512,2,128]{0,2,1:T(8,128)(2,1)S(1)}, bf16[512,2,128]{0,2,1:T(8,128)(2,1)S(1)}, u32[]{:S(2)}, u32[]{:S(2)}) collective-permute-start(bf16[512,2,128]{0,2,1:T(8,128)(2,1)S(1)} %bitcast.127), channel_id=1, source_target_pairs={{0,8},{4,12},{8,16},{12,20},{16,24},{20,28},{24,32},{28,36},{32,40... | collective-permute-start | bytes 786440 | tf_op jit(solution)/shard_map/ppermute | solution.py:17
  208.9 5.1 %collective-permute-start.1 = (bf16[512,2,128]{0,2,1:T(8,128)(2,1)S(1)}, bf16[512,2,128]{0,2,1:T(8,128)(2,1)S(1)}, u32[]{:S(2)}, u32[]{:S(2)}) collective-permute-start(bf16[512,2,128]{0,2,1:T(8,128)(2,1)S(1)} %bitcast.128), channel_id=1, source_target_pairs={{0,12},{4,16},{8,20},{12,24},{16,28},{20,32},{24,36},{28,40},{32,4... | collective-permute-start | bytes 786440 | tf_op jit(solution)/shard_map/ppermute | solution.py:17
  215.7 3.8 %collective-permute-start = (bf16[512,2,128]{0,2,1:T(8,128)(2,1)S(1)}, bf16[512,2,128]{0,2,1:T(8,128)(2,1)S(1)}, u32[]{:S(2)}, u32[]{:S(2)}) collective-permute-start(bf16[512,2,128]{0,2,1:T(8,128)(2,1)S(1)} %bitcast.129), channel_id=1, source_target_pairs={{0,16},{4,20},{8,24},{12,28},{16,32},{20,36},{24,40},{28,44},{32,4... | collective-permute-start | bytes 786440 | tf_op jit(solution)/shard_map/ppermute | solution.py:17
  223.5 3.6 %bitcast_dynamic-update-slice_fusion.4 = f32[4,512,2560]{1,2,0:T(8,128)} fusion(bf16[512,4,128]{2,0,1:T(8,128)(2,1)S(1)} %get-tuple-element.14, bf16[512,2,128]{2,0,1:T(8,128)(2,1)} %collective-permute-done.4), kind=kOutput, calls=%fused_computation.24 | convolution fusion | flops 268435456 | bytes 4849664 | tf_op jit(solution)/shard_map/qgd,kd->gqk/dot_general | solution.py:150
  227.1 3.6 %bitcast_dynamic-update-slice_fusion.3 = f32[4,512,2560]{1,2,0:T(8,128)} fusion(f32[4,512,2560]{1,2,0:T(8,128)} %bitcast_dynamic-update-slice_fusion.4, bf16[512,4,128]{2,0,1:T(8,128)(2,1)S(1)} %get-tuple-element.14, bf16[512,2,128]{2,0,1:T(8,128)(2,1)} %collective-permute-done.5), kind=kOutput, calls=%fused_computation.23 | convolution fusion | flops 268435456 | bytes 4849664 | tf_op jit(solution)/shard_map/qgd,kd->gqk/dot_general | solution.py:150
  230.8 3.6 %bitcast_dynamic-update-slice_fusion.2 = f32[4,512,2560]{1,2,0:T(8,128)} fusion(f32[4,512,2560]{1,2,0:T(8,128)} %bitcast_dynamic-update-slice_fusion.3, bf16[512,4,128]{2,0,1:T(8,128)(2,1)S(1)} %get-tuple-element.14, bf16[512,2,128]{2,0,1:T(8,128)(2,1)} %collective-permute-done.6), kind=kOutput, calls=%fused_computation.22 | convolution fusion | flops 268435456 | bytes 4849664 | tf_op jit(solution)/shard_map/qgd,kd->gqk/dot_general | solution.py:150
  234.4 3.7 %bitcast_dynamic-update-slice_fusion.1 = f32[4,512,2560]{1,2,0:T(8,128)} fusion(f32[4,512,2560]{1,2,0:T(8,128)} %bitcast_dynamic-update-slice_fusion.2, bf16[512,4,128]{2,0,1:T(8,128)(2,1)S(1)} %get-tuple-element.14, bf16[512,2,128]{2,0,1:T(8,128)(2,1)} %collective-permute-done.7), kind=kOutput, calls=%fused_computation.21 | convolution fusion | flops 268435456 | bytes 4849664 | tf_op jit(solution)/shard_map/qgd,kd->gqk/dot_general | solution.py:150
  238.1 2.7 bitcast_dynamic-update-slice_fusion
  240.8 3.0 %fusion = f32[4,512]{1,0:T(4,128)S(1)} fusion(f32[4,512,2560]{1,2,0:T(8,128)S(1)} %bitcast_dynamic-update-slice_fusion.5, pred[512,2560]{0,1:T(8,128)(4,1)S(1)} %compare_and_fusion), kind=kLoop, calls=%fused_computation.4 | loop fusion | flops 15726592 | bytes 22290432 | tf_op jit(solution)/shard_map/reduce_max | solution.py:157
  243.8 10.6 %fusion.2 = (f32[4,512]{1,0:T(4,128)S(1)}, f32[4,512]{1,0:T(4,128)S(1)}) fusion(f32[4,512,2560]{1,2,0:T(8,128)S(1)} %bitcast_dynamic-update-slice_fusion.5, f32[4,512]{1,0:T(4,128)S(1)} %fusion, pred[512,2560]{0,1:T(8,128)(4,1)S(1)} %compare_and_fusion, f32[4,512,2560]{1,2,0:T(8,128)} %bitcast_dynamic-update-slice_fusion), kind=kLoop, calls=%fused_computation.6 | loop fusion | flops 36696064 | bytes 43278336 | tf_op jit(solution)/shard_map/reduce_sum | solution.py:159
  254.5 9.5 %fusion.4 = f32[4,512]{1,0:T(4,128)S(1)} fusion(f32[4,512,2560]{1,2,0:T(8,128)} %bitcast_dynamic-update-slice_fusion, f32[4,512]{1,0:T(4,128)S(1)} %get-tuple-element.6, pred[512,2560]{0,1:T(8,128)(4,1)S(1)} %compare_and_fusion), kind=kLoop, calls=%fused_computation.8 | loop fusion | flops 20969472 | bytes 22298624 | tf_op jit(solution)/shard_map/reduce_sum | solution.py:159
  265.1 6.5 %divide_convert_fusion.1 = bf16[512,4,128]{0,2,1:T(8,128)(2,1)} fusion(f32[4,512,2560]{1,2,0:T(8,128)S(1)} %bitcast_dynamic-update-slice_fusion.5, f32[4,512]{1,0:T(4,128)S(1)} %fusion, pred[512,2560]{0,1:T(8,128)(4,1)S(1)} %compare_and_fusion, bf16[2560,2,128]{0,2,1:T(8,128)(2,1)S(1)} %constant_dynamic-update-slice_fusion, f32[512,4]{0,1:T(4,128)S(1)} %bitcast.132), kind=kOutput, calls=%fused_computation.50 | convolution fusion | flops 1363673088 | bytes 23478272 | tf_op jit(solution)/shard_map/gqk,kd->qgd/dot_general | solution.py:161
  271.6 10.2 %divide_convert_fusion = bf16[512,4,128]{0,2,1:T(8,128)(2,1)S(1)} fusion(f32[4,512,2560]{1,2,0:T(8,128)} %bitcast_dynamic-update-slice_fusion, f32[4,512]{1,0:T(4,128)S(1)} %get-tuple-element.6, pred[512,2560]{0,1:T(8,128)(4,1)S(1)} %compare_and_fusion, bf16[2560,2,128]{0,2,1:T(8,128)(2,1)} %copy-done.14, f32[512,4]{0,1:T(4,128)S(1)} %bitcast.131), kind=kOutput, calls=%fused_computation.49 | convolution fusion | flops 1363673088 | bytes 23478272 | tf_op jit(solution)/shard_map/gqk,kd->qgd/dot_general | solution.py:161
  (91 shorter events, 24.0 us)
Async XLA Ops:
  6.5 124.7 %copy-start = (bf16[4096,256]{1,0:T(8,128)(2,1)S(1)}, bf16[4096,256]{1,0:T(8,128)(2,1)}, u32[]{:S(2)}) copy-start(bf16[4096,256]{1,0:T(8,128)(2,1)} %param.15) | copy-start | bytes 6291460
  6.5 9.5 %copy-start.16 = (s32[16]{0:T(128)S(1)}, s32[16]{0:T(128)}, u32[]{:S(2)}) copy-start(s32[16]{0:T(128)} %param.21) | copy-start | bytes 196
  6.5 118.9 %all-reduce.3.cloned.1.call-start = ((), (), s32[]{:S(2)}) async-start(), calls=%async_computation.2 | async-start | bytes 3407872 | tf_op jit(solution)/shard_map/psum | solution.py:81
  11.7 113.7 %copy-start.15 = (f32[4096]{0:T(1024)S(1)}, f32[4096]{0:T(1024)}, u32[]{:S(2)}) copy-start(f32[4096]{0:T(1024)} %param.13) | copy-start | bytes 49156
  16.0 149.0 %all-gather.3.cloned.1.call-start = ((), (), s32[]{:S(2)}) async-start(), calls=%async_computation | async-start | bytes 2621440 | tf_op jit(solution)/shard_map/all_gather | solution.py:97
  125.4 65.0 %all-gather.5.cloned.1.call-start = ((), (), s32[]{:S(2)}) async-start(), calls=%async_computation.1 | async-start | bytes 2621440 | tf_op jit(solution)/shard_map/all_gather | solution.py:96
  129.3 1.9 copy-start.2
  134.2 4.9 %copy-start.8 = (f32[512,64]{1,0:T(8,128)}, f32[512,64]{1,0:T(8,128)S(1)}, u32[]{:S(2)}) copy-start(f32[512,64]{1,0:T(8,128)S(1)} %get-tuple-element.21) | copy-start | bytes 393220
  134.2 8.7 %copy-start.10 = (f32[512,64]{1,0:T(8,128)}, f32[512,64]{1,0:T(8,128)S(1)}, u32[]{:S(2)}) copy-start(f32[512,64]{1,0:T(8,128)S(1)} %get-tuple-element.22) | copy-start | bytes 393220
  134.4 0.7 copy-start.4
  134.4 1.6 copy-start.6
  136.0 85.1 %collective-permute-start.7 = (bf16[512,2,128]{2,0,1:T(8,128)(2,1)}, bf16[512,2,128]{2,0,1:T(8,128)(2,1)}, u32[]{:S(2)}, u32[]{:S(2)}) collective-permute-start(bf16[512,2,128]{2,0,1:T(8,128)(2,1)} %pad_maximum_fusion.2), channel_id=1, source_target_pairs={{0,4},{4,8},{8,12},{12,16},{16,20},{20,24},{24,28},{28,32},{32,36}... | collective-permute-start | bytes 786440 | tf_op jit(solution)/shard_map/ppermute | solution.py:17
  139.1 76.6 %collective-permute-start.6 = (bf16[512,2,128]{2,0,1:T(8,128)(2,1)}, bf16[512,2,128]{2,0,1:T(8,128)(2,1)}, u32[]{:S(2)}, u32[]{:S(2)}) collective-permute-start(bf16[512,2,128]{2,0,1:T(8,128)(2,1)} %pad_maximum_fusion.2), channel_id=1, source_target_pairs={{0,8},{4,12},{8,16},{12,20},{16,24},{20,28},{24,32},{28,36},{32,40... | collective-permute-start | bytes 786440 | tf_op jit(solution)/shard_map/ppermute | solution.py:17
  142.9 66.0 %collective-permute-start.5 = (bf16[512,2,128]{2,0,1:T(8,128)(2,1)}, bf16[512,2,128]{2,0,1:T(8,128)(2,1)}, u32[]{:S(2)}, u32[]{:S(2)}) collective-permute-start(bf16[512,2,128]{2,0,1:T(8,128)(2,1)} %pad_maximum_fusion.2), channel_id=1, source_target_pairs={{0,12},{4,16},{8,20},{12,24},{16,28},{20,32},{24,36},{28,40},{32,4... | collective-permute-start | bytes 786440 | tf_op jit(solution)/shard_map/ppermute | solution.py:17
  147.9 56.3 %collective-permute-start.4 = (bf16[512,2,128]{2,0,1:T(8,128)(2,1)}, bf16[512,2,128]{2,0,1:T(8,128)(2,1)}, u32[]{:S(2)}, u32[]{:S(2)}) collective-permute-start(bf16[512,2,128]{2,0,1:T(8,128)(2,1)} %pad_maximum_fusion.2), channel_id=1, source_target_pairs={{0,16},{4,20},{8,24},{12,28},{16,32},{20,36},{24,40},{28,44},{32,4... | collective-permute-start | bytes 786440 | tf_op jit(solution)/shard_map/ppermute | solution.py:17
  150.2 6.5 %copy-start.3 = (bf16[512,4096]{1,0:T(8,128)(2,1)S(1)}, bf16[512,4096]{1,0:T(8,128)(2,1)}, u32[]{:S(2)}) copy-start(bf16[512,4096]{1,0:T(8,128)(2,1)} %copy-done.2) | copy-start | bytes 12582916
  172.6 91.5 %collective-permute-start.3 = (bf16[512,2,128]{0,2,1:T(8,128)(2,1)}, bf16[512,2,128]{0,2,1:T(8,128)(2,1)}, u32[]{:S(2)}, u32[]{:S(2)}) collective-permute-start(bf16[512,2,128]{0,2,1:T(8,128)(2,1)} %bitcast.126), channel_id=1, source_target_pairs={{0,4},{4,8},{8,12},{12,16},{16,20},{20,24},{24,28},{28,32},{32,36}... | collective-permute-start | bytes 786440 | tf_op jit(solution)/shard_map/ppermute | solution.py:17
  201.7 1.0 copy-start.9
  201.7 1.0 copy-start.11
  202.7 1.4 copy-start.13
  204.2 59.9 %collective-permute-start.2 = (bf16[512,2,128]{0,2,1:T(8,128)(2,1)S(1)}, bf16[512,2,128]{0,2,1:T(8,128)(2,1)S(1)}, u32[]{:S(2)}, u32[]{:S(2)}) collective-permute-start(bf16[512,2,128]{0,2,1:T(8,128)(2,1)S(1)} %bitcast.127), channel_id=1, source_target_pairs={{0,8},{4,12},{8,16},{12,20},{16,24},{20,28},{24,32},{28,36},{32,40... | collective-permute-start | bytes 786440 | tf_op jit(solution)/shard_map/ppermute | solution.py:17
  208.9 55.1 %collective-permute-start.1 = (bf16[512,2,128]{0,2,1:T(8,128)(2,1)S(1)}, bf16[512,2,128]{0,2,1:T(8,128)(2,1)S(1)}, u32[]{:S(2)}, u32[]{:S(2)}) collective-permute-start(bf16[512,2,128]{0,2,1:T(8,128)(2,1)S(1)} %bitcast.128), channel_id=1, source_target_pairs={{0,12},{4,16},{8,20},{12,24},{16,28},{20,32},{24,36},{28,40},{32,4... | collective-permute-start | bytes 786440 | tf_op jit(solution)/shard_map/ppermute | solution.py:17
  215.7 7.1 %copy-start.5 = (bf16[512,2,64]{2,0,1:T(8,128)(2,1)S(1)}, bf16[512,2,64]{2,0,1:T(8,128)(2,1)}, u32[]{:S(2)}) copy-start(bf16[512,2,64]{2,0,1:T(8,128)(2,1)} %copy-done.4) | copy-start | bytes 393220
  215.7 7.1 %copy-start.7 = (bf16[512,2,64]{2,0,1:T(8,128)(2,1)S(1)}, bf16[512,2,64]{2,0,1:T(8,128)(2,1)}, u32[]{:S(2)}) copy-start(bf16[512,2,64]{2,0,1:T(8,128)(2,1)} %copy-done.6) | copy-start | bytes 393220
  215.7 48.2 %collective-permute-start = (bf16[512,2,128]{0,2,1:T(8,128)(2,1)S(1)}, bf16[512,2,128]{0,2,1:T(8,128)(2,1)S(1)}, u32[]{:S(2)}, u32[]{:S(2)}) collective-permute-start(bf16[512,2,128]{0,2,1:T(8,128)(2,1)S(1)} %bitcast.129), channel_id=1, source_target_pairs={{0,16},{4,20},{8,24},{12,28},{16,32},{20,36},{24,40},{28,44},{32,4... | collective-permute-start | bytes 786440 | tf_op jit(solution)/shard_map/ppermute | solution.py:17
  265.1 6.5 %copy-start.14 = (bf16[2560,2,128]{0,2,1:T(8,128)(2,1)}, bf16[2560,2,128]{0,2,1:T(8,128)(2,1)S(1)}, u32[]{:S(2)}) copy-start(bf16[2560,2,128]{0,2,1:T(8,128)(2,1)S(1)} %constant_dynamic-update-slice_fusion) | copy-start | bytes 3932164
  271.6 10.2 %copy-start.12 = (bf16[512,4,128]{0,2,1:T(8,128)(2,1)S(1)}, bf16[512,4,128]{0,2,1:T(8,128)(2,1)}, u32[]{:S(2)}) copy-start(bf16[512,4,128]{0,2,1:T(8,128)(2,1)} %divide_convert_fusion.1) | copy-start | bytes 1572868
  271.6 11.6 %copy-start.1 = (bf16[4096,256]{1,0:T(8,128)(2,1)S(1)}, bf16[4096,256]{1,0:T(8,128)(2,1)}, u32[]{:S(2)}) copy-start(bf16[4096,256]{1,0:T(8,128)(2,1)} %param.15) | copy-start | bytes 6291460
Sparse Core Ops, SparseCore 0:
  16.1 109.2 all-reduce.2
  127.1 30.7 all-gather.2
  159.5 30.9 all-gather.4
where the time goes:
time: 291 us; the launch traced here: 290 us
  waiting for transfers between devices  121 us (42%)
  matrix products  73.8 us (25%)
  other arithmetic  36.3 us (12%)
  starting transfers between devices  29.2 us (10%)
  local copies, waits for them, and re-layouts  16.2 us (6%)
  between operations  13.6 us (5%)
    psum x1, waiting for transfers between devices, body(): lax.psum(selector(query_up_maps).astype(jnp.bfloat16), 'tok')  106 us
    ppermute x8, starting transfers between devices, from_behind(): return lax.ppermute(x, axis, pairs)  29.2 us
    dot_general x10, matrix products, dense_scores(): jnp.einsum('qgd,kd->gqk', q_group, block_keys, preferred_element_type=jnp...  24.5 us
    reduce_sum x2, other arithmetic, body(): totals = jnp.sum(weights, axis=-1)  20.2 us
    dot_general x2, matrix products, body(): jnp.einsum('gqk,kd->qgd', probs, all_values[:, kv_group, :], preferred_el...  16.6 us
    all_gather x1, waiting for transfers between devices, body(): lax.all_gather(query_down_table, 'mlp', axis=2, tiled=True)  14.5 us
    dot_general x1, matrix products, body(): jnp.dot(normed_input, query_weight, preferred_element_type=jnp.float32)  8.29 us
    dot_general x4, matrix products, selector(): jnp.einsum('th,hrc->trc', picker, stored, preferred_element_type=jnp.floa...  6.56 us
  transfers between devices with their start and end apart: 11, of which 2 were waited for; matrix products, arithmetic and copies ran while one was open for 33% of the time, Pallas kernels for 0%

commit v1 on v0

--- a/solution.py
+++ b/solution.py
@@ -75,10 +75,11 @@
     def selector(stored):
         return jnp.einsum("th,hrc->trc", picker, stored, preferred_element_type=jnp.float32)
 
+    see_the_masks = lambda x_part: jnp.sum(lax.all_gather(x_part, "tok"), axis=0)
     summed = (
         lax.psum(selector(query_down_maps).astype(jnp.bfloat16), "tok").astype(jnp.float32),
         lax.psum(selector(value_down_maps).astype(jnp.bfloat16), "tok").astype(jnp.float32),
-        lax.psum(selector(query_up_maps).astype(jnp.bfloat16), "tok").astype(jnp.float32),
+        see_the_masks(selector(query_up_maps).astype(jnp.bfloat16)).astype(jnp.float32),
         lax.psum(selector(value_up_maps).astype(jnp.bfloat16), "tok").astype(jnp.float32),
     )
     query_down_table = summed[0].astype(jnp.bfloat16)

time: 291 us -> 365 us (1.25)
  waiting for transfers between devices: 121 us -> 179 us
  other arithmetic: 36.3 us -> 45.1 us
  local copies, waits for them, and re-layouts: 16.2 us -> 24 us
    all_gather x0 -> x1, waiting for transfers between devices: none -> 58.7 us  [body(): lax.all_gather(x_part, 'tok')]
    reduce_sum x0 -> x1, other arithmetic: none -> 9.96 us  [body(): jnp.sum(lax.all_gather(x_part, 'tok'), axis=0)]
    unnamed x41 -> x45, local copies, waits for them, and re-layouts: 6.52 us -> 11.6 us
  transfers between devices with their start and end apart: 11 -> 12, of which waited for: 2 -> 3; matrix products, arithmetic and copies ran while one was open for 33% -> 19% of each run, Pallas kernels for 0% -> 0%
where the time goes in v1:
time: 365 us; the launch traced here: 364 us
  waiting for transfers between devices  179 us (49%)
  matrix products  73.7 us (20%)
  other arithmetic  45.1 us (12%)
  starting transfers between devices  28.7 us (8%)
  local copies, waits for them, and re-layouts  24 us (7%)
  between operations  13.6 us (4%)
    psum x1, waiting for transfers between devices, body(): lax.psum(selector(query_down_maps).astype(jnp.bfloat16), 'tok')  108 us
    all_gather x1, waiting for transfers between devices, body(): lax.all_gather(x_part, 'tok')  58.7 us
    ppermute x8, starting transfers between devices, from_behind(): return lax.ppermute(x, axis, pairs)  28.6 us
    dot_general x10, matrix products, dense_scores(): jnp.einsum('qgd,kd->gqk', q_group, block_keys, preferred_element_type=jnp...  24.6 us
    reduce_sum x2, other arithmetic, body(): totals = jnp.sum(weights, axis=-1)  20.4 us
    dot_general x2, matrix products, body(): jnp.einsum('gqk,kd->qgd', probs, all_values[:, kv_group, :], preferred_el...  17.8 us
    unnamed x45, local copies, waits for them, and re-layouts  11.6 us
    all_gather x1, waiting for transfers between devices, body(): lax.all_gather(query_down_table, 'mlp', axis=2, tiled=True)  11 us
  transfers between devices with their start and end apart: 12, of which 3 were waited for; matrix products, arithmetic and copies ran while one was open for 19% of the time, Pallas kernels for 0%

profile of v1, /device:TPU:1, one launch (start us, length us, event | category | flops | bytes accessed | tf_op | source)
XLA Modules:
  0.0 364.0 jit_solution(2617427261857559917)
XLA Ops:
  9.3 2.1 convolution_convert_fusion.1
  11.4 2.1 convolution_convert_fusion.2
  13.6 108.3 %all-reduce.3.cloned.1.call-done = (bf16[16,16,1024]{2,0,1:T(8,128)(2,1)}, bf16[256,256]{1,0:T(8,128)(2,1)}, bf16[16,16,1024]{2,0,1:T(8,128)(2,1)}) async-done(((bf16[16,16,1024]{2,0,1:T(8,128)(2,1)}, bf16[256,256]{1,0:T(8,128)(2,1)}, bf16[16,16,1024]{2,0,1:T(8,128)(2,1)}), (bf16[16,16,1024]{2,0,1:T(8,128)(2,1)}, bf16[256,256]{1,0:T(8,128)(2,1)}, ...) | async-done | bytes 1179664 | tf_op jit(solution)/shard_map/psum | solution.py:80
  124.2 3.2 fusion.12
  136.0 3.1 collective-permute-start.7
  139.1 3.8 %collective-permute-start.6 = (bf16[512,2,128]{2,0,1:T(8,128)(2,1)}, bf16[512,2,128]{2,0,1:T(8,128)(2,1)}, u32[]{:S(2)}, u32[]{:S(2)}) collective-permute-start(bf16[512,2,128]{2,0,1:T(8,128)(2,1)} %pad_maximum_fusion.2), channel_id=1, source_target_pairs={{0,8},{4,12},{8,16},{12,20},{16,24},{20,28},{24,32},{28,36},{32,40... | collective-permute-start | bytes 786440 | tf_op jit(solution)/shard_map/ppermute | solution.py:17
  143.2 4.4 %fusion.61 = f32[512,256]{0,1:T(8,128)S(1)} fusion(bf16[512,4096]{1,0:T(8,128)(2,1)} %copy-done.3, bf16[4096,256]{1,0:T(8,128)(2,1)} %param.16), kind=kOutput, calls=%fused_computation.114 | convolution fusion | flops 1073741824 | bytes 6815744 | tf_op jit(solution)/shard_map/dot_general | solution.py:124
  147.6 8.3 %fusion.63 = f32[512,1024]{1,0:T(8,128)} fusion(bf16[512,4096]{1,0:T(8,128)(2,1)S(1)} %copy-done.4, bf16[4096,1024]{1,0:T(8,128)(2,1)} %param.14), kind=kOutput, calls=%fused_computation.116 | convolution fusion | flops 4294967296 | bytes 14680064 | tf_op jit(solution)/shard_map/dot_general | solution.py:115
  155.9 2.8 copy.77
  158.7 4.4 %fusion.24 = bf16[512,256]{0,1:T(8,128)(2,1)} fusion(f32[512,256]{0,1:T(8,128)S(1)} %fusion.61, bf16[256,256]{1,0:T(8,128)(2,1)S(1)} %copy-done.18, pred[512,256]{1,0:T(32,128)(4,1)S(1)} %copy.78, bf16[512,4096]{1,0:T(8,128)(2,1)} %copy-done.3, bf16[256,4096]{1,0:T(8,128)(2,1)S(1)} %bitcast.124), kind=kOutput, calls=%fused_computation.44 | convolution fusion | flops 1141506048 | bytes 7340032 | tf_op jit(solution)/shard_map/dot_general | solution.py:109
  163.1 4.5 %collective-permute-start.2 = (bf16[512,2,128]{0,2,1:T(8,128)(2,1)}, bf16[512,2,128]{0,2,1:T(8,128)(2,1)}, u32[]{:S(2)}, u32[]{:S(2)}) collective-permute-start(bf16[512,2,128]{0,2,1:T(8,128)(2,1)} %bitcast.5), channel_id=1, source_target_pairs={{0,8},{4,12},{8,16},{12,20},{16,24},{20,28},{24,32},{28,36},{32,40... | collective-permute-start | bytes 786440 | tf_op jit(solution)/shard_map/ppermute | solution.py:17
  167.6 3.0 collective-permute-start.1
  170.6 3.4 collective-permute-start
  176.0 11.0 %all-gather.7.cloned.1.call-done = bf16[16,16,4096]{2,0,1:T(8,128)(2,1)} async-done(((bf16[16,16,1024]{2,0,1:T(8,128)(2,1)}), bf16[16,16,4096]{2,0,1:T(8,128)(2,1)}) %all-gather.7.cloned.1.call-update) | async-done | bytes 2097168 | tf_op jit(solution)/shard_map/all_gather | solution.py:97
  187.0 2.7 copy.84
  189.8 3.7 %collective-permute-start.3 = (bf16[512,2,128]{0,2,1:T(8,128)(2,1)}, bf16[512,2,128]{0,2,1:T(8,128)(2,1)S(1)}, u32[]{:S(2)}, u32[]{:S(2)}) collective-permute-start(bf16[512,2,128]{0,2,1:T(8,128)(2,1)} %bitcast.5), channel_id=1, source_target_pairs={{0,4},{4,8},{8,12},{12,16},{16,20},{20,24},{24,28},{28,32},{32,36}... | collective-permute-start | bytes 786440 | tf_op jit(solution)/shard_map/ppermute | solution.py:17
  195.2 4.1 %collective-permute-start.5 = (bf16[512,2,128]{2,0,1:T(8,128)(2,1)}, bf16[512,2,128]{2,0,1:T(8,128)(2,1)}, u32[]{:S(2)}, u32[]{:S(2)}) collective-permute-start(bf16[512,2,128]{2,0,1:T(8,128)(2,1)} %pad_maximum_fusion.2), channel_id=1, source_target_pairs={{0,12},{4,16},{8,20},{12,24},{16,28},{20,32},{24,36},{28,40},{32,4... | collective-permute-start | bytes 786440 | tf_op jit(solution)/shard_map/ppermute | solution.py:17
  201.0 3.1 collective-permute-start.4
  208.3 58.7 %all-gather.9.cloned.1.call-done = bf16[512,16,1024]{2,0,1:T(8,128)(2,1)} async-done(((bf16[16,16,1024]{2,0,1:T(8,128)(2,1)}), bf16[512,16,1024]{2,0,1:T(8,128)(2,1)}) %all-gather.9.cloned.1.call-update) | async-done | bytes 16777232 | tf_op jit(solution)/shard_map/all_gather | solution.py:78
  267.1 10.0 %reduce_sum.70 = bf16[16,16,1024]{2,0,1:T(8,128)(2,1)} reduce(bf16[32,16,16,1024]{3,1,0,2:T(8,128)(2,1)} %bitcast.120, bf16[]{:T(256)} %constant.35.clone.1), dimensions={0}, to_apply=%region_8.9 | reduce | flops 8126464 | bytes 17301506 | tf_op jit(solution)/shard_map/reduce_sum | solution.py:78
  277.0 2.1 copy.87
  279.2 6.5 %add_bitcast_fusion = f32[64,8,8,128]{3,1,2,0:T(8,128)} fusion(f32[512,1024]{1,0:T(8,128)} %fusion.63, bf16[256,1024]{1,0:T(8,128)(2,1)} %bitcast.123, pred[512,256]{1,0:T(32,128)(4,1)S(1)} %copy.78, bf16[512,4096]{1,0:T(8,128)(2,1)} %copy-done.3, bf16[256,4096]{1,0:T(8,128)(2,1)S(1)} %bitcast.121), kind=kOutput, calls=%fused_computation.32 | convolution fusion | flops 1343488000 | bytes 11141120 | tf_op jit(solution)/shard_map/dot_general | solution.py:104
  297.5 3.6 bitcast_dynamic-update-slice_fusion.4
  301.1 3.6 bitcast_dynamic-update-slice_fusion.3
  304.7 3.7 %bitcast_dynamic-update-slice_fusion.2 = f32[4,512,2560]{1,2,0:T(8,128)} fusion(f32[4,512,2560]{1,2,0:T(8,128)} %bitcast_dynamic-update-slice_fusion.3, bf16[512,4,128]{2,0,1:T(8,128)(2,1)S(1)} %get-tuple-element.13, bf16[512,2,128]{2,0,1:T(8,128)(2,1)} %collective-permute-done.6), kind=kOutput, calls=%fused_computation.22 | convolution fusion | flops 268435456 | bytes 4849664 | tf_op jit(solution)/shard_map/qgd,kd->gqk/dot_general | solution.py:151
  308.4 3.7 %bitcast_dynamic-update-slice_fusion.1 = f32[4,512,2560]{1,2,0:T(8,128)} fusion(f32[4,512,2560]{1,2,0:T(8,128)} %bitcast_dynamic-update-slice_fusion.2, bf16[512,4,128]{2,0,1:T(8,128)(2,1)S(1)} %get-tuple-element.13, bf16[512,2,128]{2,0,1:T(8,128)(2,1)} %collective-permute-done.7), kind=kOutput, calls=%fused_computation.21 | convolution fusion | flops 268435456 | bytes 4849664 | tf_op jit(solution)/shard_map/qgd,kd->gqk/dot_general | solution.py:151
  312.1 2.8 bitcast_dynamic-update-slice_fusion
  314.8 3.0 fusion
  317.8 10.9 %fusion.2 = (f32[4,512]{1,0:T(4,128)S(1)}, f32[4,512]{1,0:T(4,128)S(1)}) fusion(f32[4,512,2560]{1,2,0:T(8,128)S(1)} %bitcast_dynamic-update-slice_fusion.5, f32[4,512]{1,0:T(4,128)S(1)} %fusion, pred[512,2560]{0,1:T(8,128)(4,1)S(1)} %compare_and_fusion, f32[4,512,2560]{1,2,0:T(8,128)} %bitcast_dynamic-update-slice_fusion), kind=kLoop, calls=%fused_computation.6 | loop fusion | flops 36696064 | bytes 43278336 | tf_op jit(solution)/shard_map/reduce_sum | solution.py:160
  328.7 9.5 %fusion.4 = f32[4,512]{1,0:T(4,128)S(1)} fusion(f32[4,512,2560]{1,2,0:T(8,128)} %bitcast_dynamic-update-slice_fusion, f32[4,512]{1,0:T(4,128)S(1)} %get-tuple-element.6, pred[512,2560]{0,1:T(8,128)(4,1)S(1)} %compare_and_fusion), kind=kLoop, calls=%fused_computation.8 | loop fusion | flops 20969472 | bytes 22298624 | tf_op jit(solution)/shard_map/reduce_sum | solution.py:160
  338.2 7.6 %divide_convert_fusion.1 = bf16[512,4,128]{0,2,1:T(8,128)(2,1)} fusion(f32[4,512,2560]{1,2,0:T(8,128)S(1)} %bitcast_dynamic-update-slice_fusion.5, f32[4,512]{1,0:T(4,128)S(1)} %fusion, pred[512,2560]{0,1:T(8,128)(4,1)S(1)} %compare_and_fusion, bf16[2560,2,128]{0,2,1:T(8,128)(2,1)} %constant_dynamic-update-slice_fusion, f32[512,4]{0,1:T(4,128)S(1)} %bitcast.129), kind=kOutput, calls=%fused_computation.50 | convolution fusion | flops 1363673088 | bytes 23478272 | tf_op jit(solution)/shard_map/gqk,kd->qgd/dot_general | solution.py:162
  345.9 10.1 %divide_convert_fusion = bf16[512,4,128]{0,2,1:T(8,128)(2,1)S(1)} fusion(f32[4,512,2560]{1,2,0:T(8,128)} %bitcast_dynamic-update-slice_fusion, f32[4,512]{1,0:T(4,128)S(1)} %get-tuple-element.6, pred[512,2560]{0,1:T(8,128)(4,1)S(1)} %compare_and_fusion, bf16[2560,2,128]{0,2,1:T(8,128)(2,1)} %constant_dynamic-update-slice_fusion, f32[512,4]{0,1:T(4,128)S(1)} %bitcast.128), kind=kOutput, calls=%fused_computation.49 | convolution fusion | flops 1363673088 | bytes 23478272 | tf_op jit(solution)/shard_map/gqk,kd->qgd/dot_general | solution.py:162
  (99 shorter events, 36.5 us)
Async XLA Ops:
  6.5 124.7 %copy-start = (bf16[4096,256]{1,0:T(8,128)(2,1)S(1)}, bf16[4096,256]{1,0:T(8,128)(2,1)}, u32[]{:S(2)}) copy-start(bf16[4096,256]{1,0:T(8,128)(2,1)} %param.15) | copy-start | bytes 6291460
  6.5 116.2 %copy-start.14 = (bf16[8,16,1024]{2,1,0:T(8,128)(2,1)S(1)}, bf16[8,16,1024]{2,1,0:T(8,128)(2,1)}, u32[]{:S(2)}) copy-start(bf16[8,16,1024]{2,1,0:T(8,128)(2,1)} %param.19) | copy-start | bytes 786436
  6.5 117.4 %copy-start.17 = (s32[16]{0:T(128)S(1)}, s32[16]{0:T(128)}, u32[]{:S(2)}) copy-start(s32[16]{0:T(128)} %param.21) | copy-start | bytes 196
  6.5 115.4 %all-reduce.3.cloned.1.call-start = ((), (), s32[]{:S(2)}) async-start(), calls=%async_computation.3 | async-start | bytes 2359296 | tf_op jit(solution)/shard_map/psum | solution.py:80
  11.4 116.0 %copy-start.16 = (f32[4096]{0:T(1024)S(1)}, f32[4096]{0:T(1024)}, u32[]{:S(2)}) copy-start(f32[4096]{0:T(1024)} %param.13) | copy-start | bytes 49156
  13.6 142.3 %all-gather.5.cloned.1.call-start = ((), (), s32[]{:S(2)}) async-start(), calls=%async_computation | async-start | bytes 2621440 | tf_op jit(solution)/shard_map/all_gather | solution.py:98
  122.0 65.0 %all-gather.7.cloned.1.call-start = ((), (), s32[]{:S(2)}) async-start(), calls=%async_computation.1 | async-start | bytes 2621440 | tf_op jit(solution)/shard_map/all_gather | solution.py:97
  122.7 144.3 %all-gather.9.cloned.1.call-start = ((), (), s32[]{:S(2)}) async-start(), calls=%async_computation.2 | async-start | bytes 17301504 | tf_op jit(solution)/shard_map/all_gather | solution.py:78
  124.2 3.5 copy-start.2
  129.3 1.9 copy-start.3
  133.3 14.3 %copy-start.15 = (s32[512]{0:T(512)}, s32[512]{0:T(512)S(1)}, u32[]{:S(2)}) copy-start(s32[512]{0:T(512)S(1)} %select_reduce_fusion) | copy-start | bytes 6148
  134.3 4.8 %copy-start.9 = (f32[512,64]{1,0:T(8,128)}, f32[512,64]{1,0:T(8,128)S(1)}, u32[]{:S(2)}) copy-start(f32[512,64]{1,0:T(8,128)S(1)} %get-tuple-element.20) | copy-start | bytes 393220
  134.3 4.8 %copy-start.11 = (f32[512,64]{1,0:T(8,128)}, f32[512,64]{1,0:T(8,128)S(1)}, u32[]{:S(2)}) copy-start(f32[512,64]{1,0:T(8,128)S(1)} %get-tuple-element.21) | copy-start | bytes 393220
  134.4 0.7 copy-start.5
  134.4 1.6 copy-start.7
  136.0 159.1 %collective-permute-start.7 = (bf16[512,2,128]{2,0,1:T(8,128)(2,1)}, bf16[512,2,128]{2,0,1:T(8,128)(2,1)}, u32[]{:S(2)}, u32[]{:S(2)}) collective-permute-start(bf16[512,2,128]{2,0,1:T(8,128)(2,1)} %pad_maximum_fusion.2), channel_id=1, source_target_pairs={{0,4},{4,8},{8,12},{12,16},{16,20},{20,24},{24,28},{28,32},{32,36}... | collective-permute-start | bytes 786440 | tf_op jit(solution)/shard_map/ppermute | solution.py:17
  139.1 154.3 %collective-permute-start.6 = (bf16[512,2,128]{2,0,1:T(8,128)(2,1)}, bf16[512,2,128]{2,0,1:T(8,128)(2,1)}, u32[]{:S(2)}, u32[]{:S(2)}) collective-permute-start(bf16[512,2,128]{2,0,1:T(8,128)(2,1)} %pad_maximum_fusion.2), channel_id=1, source_target_pairs={{0,8},{4,12},{8,16},{12,20},{16,24},{20,28},{24,32},{28,36},{32,40... | collective-permute-start | bytes 786440 | tf_op jit(solution)/shard_map/ppermute | solution.py:17
  143.2 4.4 %copy-start.4 = (bf16[512,4096]{1,0:T(8,128)(2,1)S(1)}, bf16[512,4096]{1,0:T(8,128)(2,1)}, u32[]{:S(2)}) copy-start(bf16[512,4096]{1,0:T(8,128)(2,1)} %copy-done.3) | copy-start | bytes 12582916
  155.9 2.8 copy-start.18
  163.1 37.9 %collective-permute-start.2 = (bf16[512,2,128]{0,2,1:T(8,128)(2,1)}, bf16[512,2,128]{0,2,1:T(8,128)(2,1)}, u32[]{:S(2)}, u32[]{:S(2)}) collective-permute-start(bf16[512,2,128]{0,2,1:T(8,128)(2,1)} %bitcast.5), channel_id=1, source_target_pairs={{0,8},{4,12},{8,16},{12,20},{16,24},{20,28},{24,32},{28,36},{32,40... | collective-permute-start | bytes 786440 | tf_op jit(solution)/shard_map/ppermute | solution.py:17
  167.6 27.6 %collective-permute-start.1 = (bf16[512,2,128]{0,2,1:T(8,128)(2,1)}, bf16[512,2,128]{0,2,1:T(8,128)(2,1)}, u32[]{:S(2)}, u32[]{:S(2)}) collective-permute-start(bf16[512,2,128]{0,2,1:T(8,128)(2,1)} %bitcast.5), channel_id=1, source_target_pairs={{0,12},{4,16},{8,20},{12,24},{16,28},{20,32},{24,36},{28,40},{32,4... | collective-permute-start | bytes 786440 | tf_op jit(solution)/shard_map/ppermute | solution.py:17
  170.6 19.2 %collective-permute-start = (bf16[512,2,128]{0,2,1:T(8,128)(2,1)}, bf16[512,2,128]{0,2,1:T(8,128)(2,1)}, u32[]{:S(2)}, u32[]{:S(2)}) collective-permute-start(bf16[512,2,128]{0,2,1:T(8,128)(2,1)} %bitcast.5), channel_id=1, source_target_pairs={{0,16},{4,20},{8,24},{12,28},{16,32},{20,36},{24,40},{28,44},{32,4... | collective-permute-start | bytes 786440 | tf_op jit(solution)/shard_map/ppermute | solution.py:17
  189.8 16.1 %collective-permute-start.3 = (bf16[512,2,128]{0,2,1:T(8,128)(2,1)}, bf16[512,2,128]{0,2,1:T(8,128)(2,1)S(1)}, u32[]{:S(2)}, u32[]{:S(2)}) collective-permute-start(bf16[512,2,128]{0,2,1:T(8,128)(2,1)} %bitcast.5), channel_id=1, source_target_pairs={{0,4},{4,8},{8,12},{12,16},{16,20},{20,24},{24,28},{28,32},{32,36}... | collective-permute-start | bytes 786440 | tf_op jit(solution)/shard_map/ppermute | solution.py:17
  195.2 96.6 %collective-permute-start.5 = (bf16[512,2,128]{2,0,1:T(8,128)(2,1)}, bf16[512,2,128]{2,0,1:T(8,128)(2,1)}, u32[]{:S(2)}, u32[]{:S(2)}) collective-permute-start(bf16[512,2,128]{2,0,1:T(8,128)(2,1)} %pad_maximum_fusion.2), channel_id=1, source_target_pairs={{0,12},{4,16},{8,20},{12,24},{16,28},{20,32},{24,36},{28,40},{32,4... | collective-permute-start | bytes 786440 | tf_op jit(solution)/shard_map/ppermute | solution.py:17
  201.0 89.1 %collective-permute-start.4 = (bf16[512,2,128]{2,0,1:T(8,128)(2,1)}, bf16[512,2,128]{2,0,1:T(8,128)(2,1)}, u32[]{:S(2)}, u32[]{:S(2)}) collective-permute-start(bf16[512,2,128]{2,0,1:T(8,128)(2,1)} %pad_maximum_fusion.2), channel_id=1, source_target_pairs={{0,16},{4,20},{8,24},{12,28},{16,32},{20,36},{24,40},{28,44},{32,4... | collective-permute-start | bytes 786440 | tf_op jit(solution)/shard_map/ppermute | solution.py:17
  287.7 1.0 copy-start.10
  287.7 1.0 copy-start.12
  293.4 3.3 copy-start.6
  293.4 3.3 copy-start.8
  345.9 10.2 %copy-start.13 = (bf16[512,4,128]{0,2,1:T(8,128)(2,1)S(1)}, bf16[512,4,128]{0,2,1:T(8,128)(2,1)}, u32[]{:S(2)}) copy-start(bf16[512,4,128]{0,2,1:T(8,128)(2,1)} %divide_convert_fusion.1) | copy-start | bytes 1572868
  345.9 11.6 %copy-start.1 = (bf16[4096,256]{1,0:T(8,128)(2,1)S(1)}, bf16[4096,256]{1,0:T(8,128)(2,1)}, u32[]{:S(2)}) copy-start(bf16[4096,256]{1,0:T(8,128)(2,1)} %param.15) | copy-start | bytes 6291460
Sparse Core Ops, SparseCore 0:
  13.7 108.2 all-reduce.2
  123.6 30.7 all-gather.4
  156.1 30.9 all-gather.6
  189.2 77.8 all-gather.8
